TPU v7x, 256 devices: a whole 4x4x8 slice. The times are simulated.
256 devices in a mesh: prow: 16 (over y_hi, z), pcol: 16 (over x, y_lo, core).
Axes of the slice: x: 4, y: 4 (y_hi: 2, y_lo: 2; y = y_hi * 2 + y_lo), z: 8, core: 2. Of those that a mesh axis runs over, the one named last changes fastest.
Arguments:
- ainv: float32 [20480, 20480], P('prow', 'pcol'), may hold values from -0.15625 to 0.15625
- panels: float32 [3, 20480, 512], P(None, ('prow', 'pcol')), may hold values from -0.8 to 0.8
- ancestors: int32 [3, 2560], P(None, ('prow', 'pcol')), may hold values from 0 to 1, as said below
- dinv: float32 [3, 512, 512], P(None, 'prow', 'pcol'), may hold values from -6 to 6
Outputs:
- u_panel: float32 [3, 20480, 512], P(None, ('prow', 'pcol'))
- diag: float32 [3, 512, 512], P(None, 'prow', 'pcol')
Inputs may be any that keep to these rules, and one draw needn't show every extreme that they name: `ancestors`: each entry is 0 or 1; the share of ancestor blocks varies strongly between regions of the rows.
All inputs are finite; a program needn't handle non-finite values.
Results may differ from a plain program's by a relative error of at most 0.00007.
Values sent between devices are 32-bit elements; how exact they have to be, the bound alone decides.
A program may use at most 128 MiB of HBM per device.

v0:
```python
import jax
import jax.numpy as jnp
from jax import lax
from jax.sharding import Mesh
from jax.sharding import PartitionSpec as P

S = 512
NSUP = 3
BLK = 8
PCOL = ("pcol_0", "pcol_1", "pcol_2")
PROW_PCOL = ("prow", "pcol_0", "pcol_1", "pcol_2")


def split_up(value, dim, peers):
    before, after = (value.shape[:dim], value.shape[dim + 1 :])
    return jnp.moveaxis(value.reshape(*before, peers, -1, *after), dim, 0)


def sum_by_chip(value, chips, core, dim):
    sizes = (lax.axis_size(chips), lax.axis_size(core))
    tiles = split_up(value, dim, sizes[0] * sizes[1])
    inside = tiles.shape[1:]
    tiles = tiles.reshape(*sizes, *inside).swapaxes(0, 1).reshape(-1, *inside)
    tiles = lax.psum_scatter(tiles, core, scatter_dimension=0, tiled=True)
    return lax.psum_scatter(tiles, chips, scatter_dimension=0, tiled=True)[0]


def sent_and_summed(value, axis, dim):
    peers = lax.axis_size(axis)
    tiles = lax.all_to_all(split_up(value, dim, peers), axis, 0, 0, tiled=True)
    return jnp.sum(tiles, axis=0)


def apply_rows(columns, piece):

    def dense_product():
        return jnp.dot(columns, piece, precision=lax.Precision.HIGHEST)

    def no_product():
        return jnp.zeros((columns.shape[0], piece.shape[1]), jnp.float32)

    return lax.cond(jnp.any(piece != 0.0), dense_product, no_product)


def on_device(ainv, panels, ancestors, dinv):
    row_flags = jnp.repeat(ancestors, BLK, axis=1).astype(jnp.float32)
    masked = panels * row_flags[:, :, None]
    local_rows = ainv.shape[0]
    empty = jnp.zeros((NSUP, local_rows, S), jnp.float32)
    total = empty
    piece = lax.all_gather(masked, "prow", axis=1, tiled=True)
    for member in range(NSUP):
        total = total.at[member].add(apply_rows(ainv, piece[member]))
    partial_value = sum_by_chip(total, ("pcol_0", "pcol_1"), "pcol_2", 1)
    u_panel = -(row_flags[:, :, None] * partial_value)
    local_terms = jnp.einsum("srn,srm->snm", masked, u_panel, precision=lax.Precision.HIGHEST)
    by_columns = sent_and_summed(local_terms, PCOL, 2)
    own_block = sent_and_summed(by_columns, "prow", 1)
    diag = dinv - own_block
    return (u_panel, diag)


def solution(mesh):
    split = Mesh(
        mesh.devices.reshape(mesh.shape["prow"], 4, 2, 2), ("prow", "pcol_0", "pcol_1", "pcol_2")
    )
    in_specs = (
        P("prow", PCOL),
        P(None, PROW_PCOL, None),
        P(None, PROW_PCOL),
        P(None, "prow", PCOL),
    )
    out_specs = (P(None, PROW_PCOL, None), P(None, "prow", PCOL))
    return jax.shard_map(
        on_device, mesh=split, in_specs=in_specs, out_specs=out_specs, check_vma=False
    )
```

profile of v0, /device:TPU:32, one launch (start us, length us, event | category | flops | bytes accessed | tf_op | source)
XLA Modules:
  0.0 404.4 jit_solution(11009436670930716270)
XLA Ops:
  7.2 0.7 convert_element_type.20
  8.0 0.1 convert_element_type.21
  8.1 1.9 broadcast_multiply_fusion
  10.0 132.6 %all-gather.2.cloned.1.call-done = f32[3,1280,512]{2,1,0:T(8,128)} async-done(((f32[3,80,512]{2,1,0:T(8,128)}), f32[3,1280,512]{2,1,0:T(8,128)}) %all-gather.2.cloned.1.call-update) | async-done | bytes 7864336 | tf_op jit(solution)/shard_map/all_gather | solution.py:51
  142.6 5.0 %compare_reduce_fusion = (pred[]{:T(512)}, pred[]{:T(512)}, pred[]{:T(512)}) fusion(f32[3,1280,512]{2,1,0:T(8,128)} %all-gather.2.cloned.1.call-done), kind=kLoop, calls=%fused_computation.9 | loop fusion | flops 3932157 | bytes 7864323 | tf_op jit(solution)/shard_map/reduce_or | solution.py:42
  149.6 6.7 %slice_bitcast_fusion = (f32[1280,512]{1,0:T(8,128)}, f32[1280,512]{1,0:T(8,128)}, f32[1280,512]{1,0:T(8,128)}) fusion(f32[3,1280,512]{2,1,0:T(8,128)} %all-gather.2.cloned.1.call-done), kind=kLoop, calls=%fused_computation.4 | loop fusion | bytes 15728640 | tf_op jit(solution)/shard_map/squeeze | solution.py:53
  156.2 13.4 %conditional.4 = (f32[1,1280,512]{2,1,0:T(8,128)S(1)}) conditional(s32[]{:T(128)} %convert_element_type.23, () %tuple.46, (f32[1280,1280]{1,0:T(8,128)}, f32[1280,512]{1,0:T(8,128)}) %tuple.47), branch_computations={%region_4.0_spmd, %region_5.0_spmd} | conditional | flops 10066329600 | bytes 11796488 | solution.py:42
  156.2 13.4 %convolution_bitcast_fusion.1 = f32[1,1280,512]{2,1,0:T(8,128)S(1)} fusion(f32[1280,1280]{1,0:T(8,128)} %get-tuple-element.62, f32[1280,512]{1,0:T(8,128)} %get-tuple-element.63), kind=kOutput, calls=%fused_computation.1 | convolution fusion | flops 10066329600 | bytes 11796480 | tf_op jit(solution)/shard_map/cond/branch_1_fun/dot_general | solution.py:37
  169.6 17.6 %conditional.3 = (f32[3,1280,512]{2,1,0:T(8,128)}) conditional(s32[]{:T(128)} %convert_element_type.22, () %tuple.44, (f32[1280,1280]{1,0:T(8,128)}, f32[1280,512]{1,0:T(8,128)}) %tuple.45), branch_computations={%region_1.0_spmd, %region_2.0_spmd} | conditional | flops 10066329600 | bytes 22282252 | solution.py:42
  169.8 13.4 %convolution_bitcast_fusion = f32[1,1280,512]{2,1,0:T(8,128)S(1)} fusion(f32[1280,1280]{1,0:T(8,128)} %get-tuple-element.60, f32[1280,512]{1,0:T(8,128)} %get-tuple-element.61), kind=kOutput, calls=%fused_computation | convolution fusion | flops 10066329600 | bytes 11796480 | tf_op jit(solution)/shard_map/cond/branch_1_fun/dot_general | solution.py:37
  183.3 4.0 scatter-add.9
  187.3 1.8 constant_dynamic-update-slice_fusion
  189.0 13.4 %conditional.5 = (f32[1,1280,512]{2,1,0:T(8,128)S(1)}) conditional(s32[]{:T(128)} %convert_element_type.24, () %tuple.48, (f32[1280,1280]{1,0:T(8,128)}, f32[1280,512]{1,0:T(8,128)}) %tuple.49), branch_computations={%region_7.0_spmd, %region_8.0_spmd} | conditional | flops 10066329600 | bytes 11796488 | solution.py:42
  189.0 13.4 %convolution_bitcast_fusion.2 = f32[1,1280,512]{2,1,0:T(8,128)S(1)} fusion(f32[1280,1280]{1,0:T(8,128)} %get-tuple-element.64, f32[1280,512]{1,0:T(8,128)} %get-tuple-element.65), kind=kOutput, calls=%fused_computation.2 | convolution fusion | flops 10066329600 | bytes 11796480 | tf_op jit(solution)/shard_map/cond/branch_1_fun/dot_general | solution.py:37
  202.4 3.9 fusion
  206.3 8.0 %copy.9 = f32[2,8,3,80,512]{4,3,2,1,0:T(8,128)} copy(f32[2,8,3,80,512]{4,3,0,1,2:T(8,128)} %bitcast.45) | data formatting | bytes 15728640 | tf_op jit(solution)/shard_map/transpose | solution.py:23
  214.3 0.3 reduce-scatter.5.cloned.1.call-start
  214.6 20.3 %reduce-scatter.3.cloned.1.call-done = f32[8,3,80,512]{3,2,1,0:T(8,128)} async-done(((f32[16,3,80,512]{3,2,1,0:T(8,128)}), f32[8,3,80,512]{3,2,1,0:T(8,128)}) %reduce-scatter.3.cloned.1.call-update) | async-done | bytes 3932176 | tf_op jit(solution)/shard_map/reduce_scatter | solution.py:24
  235.0 91.7 %reduce-scatter.5.cloned.1.call-done = f32[1,3,80,512]{3,2,1,0:T(8,128)} async-done(((f32[8,3,80,512]{3,2,1,0:T(8,128)}), f32[1,3,80,512]{3,2,1,0:T(8,128)}) %reduce-scatter.5.cloned.1.call-update) | async-done | bytes 491536 | tf_op jit(solution)/shard_map/reduce_scatter | solution.py:25
  326.7 1.1 fusion.1
  327.9 2.7 fusion.2
  330.6 0.5 copy.16
  331.1 43.8 %all_to_all.10 = f32[16,3,512,32]{2,3,1,0:T(8,128)S(1)} all-to-all(f32[16,3,512,32]{2,3,1,0:T(8,128)S(1)} %bitcast.48), channel_id=1, replica_groups=mesh['prow'=16,'pcol_0'=4,'pcol_1'=2,'pcol_2'=2] {'pcol_0','pcol_1','pco..., dimensions={0} | all-to-all | bytes 6291456 | tf_op jit(solution)/shard_map/all_to_all | solution.py:30
  374.9 0.3 reduce_sum.18
  375.2 0.2 reshape.129
  375.4 0.4 copy.12
  375.8 0.3 reshape.130
  376.2 19.1 %all_to_all.11 = f32[16,1,3072]{2,1,0:T(1,128)S(1)} all-to-all(f32[16,1,3072]{2,1,0:T(1,128)S(1)} %reshape.130), channel_id=1, replica_groups=mesh['prow'=16,'pcol_0'=4,'pcol_1'=2,'pcol_2'=2] {'prow'}, dimensions={0} | all-to-all | bytes 393216 | tf_op jit(solution)/shard_map/all_to_all | solution.py:30
  395.3 0.5 broadcast.77
  395.8 1.1 reduce.6
  396.9 0.2 reshape.131
  397.2 0.6 sub.3
  (13 shorter events, 0.3 us)
Async XLA Ops:
  7.2 135.5 %all-gather.2.cloned.1.call-start = ((), (), s32[]{:S(2)}) async-start(), calls=%async_computation.4 | async-start | bytes 8355840 | tf_op jit(solution)/shard_map/all_gather | solution.py:51
  10.0 224.9 %reduce-scatter.3.cloned.1.call-start = ((), (), s32[]{:S(2)}) async-start(), calls=%async_computation.5 | async-start | bytes 11796480 | tf_op jit(solution)/shard_map/reduce_scatter | solution.py:24
  214.3 113.5 %copy-start = (f32[3,80,512]{2,1,0:T(8,128)S(1)}, f32[3,80,512]{2,1,0:T(8,128)}, u32[]{:S(2)}) copy-start(f32[3,80,512]{2,1,0:T(8,128)} %broadcast_multiply_fusion) | copy-start | bytes 1474564
  214.3 112.4 %reduce-scatter.5.cloned.1.call-start = ((), (), s32[]{:S(2)}) async-start(), calls=%async_computation.6 | async-start | bytes 4423680 | tf_op jit(solution)/shard_map/reduce_scatter | solution.py:25
  327.8 2.7 copy-start.1
  375.4 21.8 %copy-start.2 = (f32[3,32,32]{2,1,0:T(8,128)S(1)}, f32[3,32,32]{2,1,0:T(8,128)}, u32[]{:S(2)}) copy-start(f32[3,32,32]{2,1,0:T(8,128)} %param.19) | copy-start | bytes 36868
Sparse Core Ops, SparseCore 0:
  11.1 131.4 all-gather.1
  214.5 20.4 reduce-scatter.2
  237.5 89.1 reduce-scatter.4
where the time goes:
time: 405 us; the launch traced here: 404 us
  waiting for transfers between devices  245 us (60%)
  blocking collectives  62.9 us (16%)
  matrix products  42.9 us (11%)
  local copies, waits for them, and re-layouts  22.8 us (6%)
  between operations  15.8 us (4%)
  other arithmetic  14.7 us (4%)
    all_gather x1, waiting for transfers between devices, on_device(): piece = lax.all_gather(masked, 'prow', axis=1, tiled=True)  133 us
    reduce_scatter x1, waiting for transfers between devices, sum_by_chip(): return lax.psum_scatter(tiles, chips, scatter_dimension=0, tiled=True)[0]  91.7 us
    all_to_all x2, blocking collectives, sent_and_summed(): tiles = lax.all_to_all(split_up(value, dim, peers), axis, 0, 0, tiled=True)  62.9 us
    dot_general x3, matrix products, dense_product(): return jnp.dot(columns, piece, precision=lax.Precision.HIGHEST)  40.2 us
    reduce_scatter x1, waiting for transfers between devices, sum_by_chip(): tiles = lax.psum_scatter(tiles, core, scatter_dimension=0, tiled=True)  20.3 us
  transfers between devices with their start and end apart: 3, of which 3 were waited for; matrix products, arithmetic and copies ran while one was open for 0% of the time, Pallas kernels for 0%

commit v1 on v0

--- a/solution.py
+++ b/solution.py
@@ -48,7 +48,9 @@
     local_rows = ainv.shape[0]
     empty = jnp.zeros((NSUP, local_rows, S), jnp.float32)
     total = empty
-    piece = lax.all_gather(masked, "prow", axis=1, tiled=True)
+    piece = jnp.concatenate(
+        lax.all_to_all(jnp.stack([masked] * lax.axis_size("prow")), "prow", 0, 0), axis=1
+    )
     for member in range(NSUP):
         total = total.at[member].add(apply_rows(ainv, piece[member]))
     partial_value = sum_by_chip(total, ("pcol_0", "pcol_1"), "pcol_2", 1)

time: 405 us -> 471 us (1.16)
  waiting for transfers between devices: 245 us -> 296 us
  starting transfers between devices: 0.34 us -> 11.5 us
    all_to_all x0 -> x1, waiting for transfers between devices: none -> 177 us  [on_device(): lax.all_to_all(jnp.stack([masked] * lax.axis_size('prow')), 'prow', 0, 0)]
    all_gather x1 -> x0, waiting for transfers between devices: 133 us -> none  [on_device(): piece = lax.all_gather(masked, 'prow', axis=1, tiled=True)]
    all_to_all x0 -> x1, starting transfers between devices: none -> 11.2 us  [on_device(): lax.all_to_all(jnp.stack([masked] * lax.axis_size('prow')), 'prow', 0, 0)]
    slice x0 -> x1, local copies, waits for them, and re-layouts: none -> 6.8 us  [on_device(): total = total.at[member].add(apply_rows(ainv, piece[member]))]
    reduce_scatter x1, waiting for transfers between devices: 20.3 us -> 27 us  [sum_by_chip(): tiles = lax.psum_scatter(tiles, core, scatter_dimension=0, tiled=True)]
    squeeze x1 -> x0, local copies, waits for them, and re-layouts: 6.65 us -> none  [on_device(): total = total.at[member].add(apply_rows(ainv, piece[member]))]
where the time goes in v1:
time: 471 us; the launch traced here: 470 us
  waiting for transfers between devices  296 us (63%)
  blocking collectives  62.9 us (13%)
  matrix products  42.9 us (9%)
  local copies, waits for them, and re-layouts  27.1 us (6%)
  between operations  16.1 us (3%)
  other arithmetic  13.9 us (3%)
  starting transfers between devices  11.5 us (2%)
    all_to_all x1, waiting for transfers between devices, on_device(): lax.all_to_all(jnp.stack([masked] * lax.axis_size('prow')), 'prow', 0, 0)  177 us
    reduce_scatter x1, waiting for transfers between devices, sum_by_chip(): return lax.psum_scatter(tiles, chips, scatter_dimension=0, tiled=True)[0]  91.8 us
    all_to_all x2, blocking collectives, sent_and_summed(): tiles = lax.all_to_all(split_up(value, dim, peers), axis, 0, 0, tiled=True)  62.9 us
    dot_general x3, matrix products, dense_product(): return jnp.dot(columns, piece, precision=lax.Precision.HIGHEST)  40.3 us
    reduce_scatter x1, waiting for transfers between devices, sum_by_chip(): tiles = lax.psum_scatter(tiles, core, scatter_dimension=0, tiled=True)  27 us
    all_to_all x1, starting transfers between devices, on_device(): lax.all_to_all(jnp.stack([masked] * lax.axis_size('prow')), 'prow', 0, 0)  11.2 us
  transfers between devices with their start and end apart: 3, of which 3 were waited for; matrix products, arithmetic and copies ran while one was open for 0% of the time, Pallas kernels for 0%

profile of v1, /device:TPU:32, one launch (start us, length us, event | category | flops | bytes accessed | tf_op | source)
XLA Modules:
  0.0 470.4 jit_solution(3059026423331615971)
XLA Ops:
  7.2 0.7 convert_element_type.20
  8.0 1.1 broadcast_multiply_fusion
  9.1 4.2 stack.2
  13.3 11.2 %all-to-all-start = ((f32[16,3,80,512]{3,2,1,0:T(8,128)}), f32[16,3,80,512]{3,2,1,0:T(8,128)}, u32[]{:S(2)}, u32[]{:S(2)}) async-start(f32[16,3,80,512]{3,2,1,0:T(8,128)} %stack.2), calls=%async_computation | async-start | bytes 15728640 | tf_op jit(solution)/shard_map/all_to_all | solution.py:52
  24.6 176.9 %all-to-all-done = f32[16,3,80,512]{3,2,1,0:T(8,128)} async-done(((f32[16,3,80,512]{3,2,1,0:T(8,128)}), f32[16,3,80,512]{3,2,1,0:T(8,128)}, u32[]{:S(2)}, u32[]{:S(2)}) %all-to-all-start) | async-done | bytes 7864352 | tf_op jit(solution)/shard_map/all_to_all | solution.py:52
  201.5 5.1 %compare_reduce_fusion = (pred[]{:T(512)}, pred[]{:T(512)}, pred[]{:T(512)}) fusion(f32[3,16,80,512]{3,2,0,1:T(8,128)} %bitcast.9), kind=kLoop, calls=%fused_computation.6 | loop fusion | flops 3932157 | bytes 7864323 | tf_op jit(solution)/shard_map/reduce_or | solution.py:42
  206.5 6.8 %fusion.2 = (f32[1,16,80,512]{3,2,0,1:T(8,128)}, f32[1,16,80,512]{3,2,0,1:T(8,128)}, f32[1,16,80,512]{3,2,0,1:T(8,128)}) fusion(f32[3,16,80,512]{3,2,0,1:T(8,128)} %bitcast.9), kind=kLoop, calls=%fused_computation.13 | loop fusion | bytes 15728640 | tf_op jit(solution)/shard_map/slice | solution.py:55
  215.3 13.4 %conditional.4 = (f32[1,1280,512]{2,1,0:T(8,128)S(1)}) conditional(s32[]{:T(128)} %convert_element_type.23, () %tuple.46, (f32[1280,1280]{1,0:T(8,128)}, f32[1,16,80,512]{3,2,0,1:T(8,128)}) %tuple.47), branch_computations={%region_4.0_spmd, %region_5.0_spmd} | conditional | flops 10066329600 | bytes 11796488 | solution.py:42
  215.3 13.4 %convolution_bitcast_fusion.1 = f32[1,1280,512]{2,1,0:T(8,128)S(1)} fusion(f32[1280,1280]{1,0:T(8,128)} %get-tuple-element.62, f32[1280,512]{1,0:T(8,128)} %bitcast.50), kind=kOutput, calls=%fused_computation.1 | convolution fusion | flops 10066329600 | bytes 11796480 | tf_op jit(solution)/shard_map/cond/branch_1_fun/dot_general | solution.py:37
  228.7 17.7 %conditional.3 = (f32[3,1280,512]{2,1,0:T(8,128)}) conditional(s32[]{:T(128)} %convert_element_type.22, () %tuple.44, (f32[1280,1280]{1,0:T(8,128)}, f32[1,16,80,512]{3,2,0,1:T(8,128)}) %tuple.45), branch_computations={%region_1.0_spmd, %region_2.0_spmd} | conditional | flops 10066329600 | bytes 22282252 | solution.py:42
  228.9 13.4 %convolution_bitcast_fusion = f32[1,1280,512]{2,1,0:T(8,128)S(1)} fusion(f32[1280,1280]{1,0:T(8,128)} %get-tuple-element.60, f32[1280,512]{1,0:T(8,128)} %bitcast.49), kind=kOutput, calls=%fused_computation | convolution fusion | flops 10066329600 | bytes 11796480 | tf_op jit(solution)/shard_map/cond/branch_1_fun/dot_general | solution.py:37
  242.4 4.1 scatter-add.9
  246.5 1.8 constant_dynamic-update-slice_fusion
  248.2 13.4 %conditional.5 = (f32[1,1280,512]{2,1,0:T(8,128)S(1)}) conditional(s32[]{:T(128)} %convert_element_type.24, () %tuple.48, (f32[1280,1280]{1,0:T(8,128)}, f32[1,16,80,512]{3,2,0,1:T(8,128)}) %tuple.49), branch_computations={%region_7.0_spmd, %region_8.0_spmd} | conditional | flops 10066329600 | bytes 11796488 | solution.py:42
  248.2 13.4 %convolution_bitcast_fusion.2 = f32[1,1280,512]{2,1,0:T(8,128)S(1)} fusion(f32[1280,1280]{1,0:T(8,128)} %get-tuple-element.64, f32[1280,512]{1,0:T(8,128)} %bitcast.48), kind=kOutput, calls=%fused_computation.2 | convolution fusion | flops 10066329600 | bytes 11796480 | tf_op jit(solution)/shard_map/cond/branch_1_fun/dot_general | solution.py:37
  261.6 3.8 fusion
  265.4 7.9 %copy.12 = f32[2,8,3,80,512]{4,3,2,1,0:T(8,128)} copy(f32[2,8,3,80,512]{4,3,0,1,2:T(8,128)} %bitcast.43) | data formatting | bytes 15728640 | tf_op jit(solution)/shard_map/transpose | solution.py:23
  273.4 0.3 reduce-scatter.5.cloned.1.call-start
  273.7 27.0 %reduce-scatter.3.cloned.1.call-done = f32[8,3,80,512]{3,2,1,0:T(8,128)} async-done(((f32[16,3,80,512]{3,2,1,0:T(8,128)}), f32[8,3,80,512]{3,2,1,0:T(8,128)}) %reduce-scatter.3.cloned.1.call-update) | async-done | bytes 3932176 | tf_op jit(solution)/shard_map/reduce_scatter | solution.py:24
  300.7 91.8 %reduce-scatter.5.cloned.1.call-done = f32[1,3,80,512]{3,2,1,0:T(8,128)} async-done(((f32[8,3,80,512]{3,2,1,0:T(8,128)}), f32[1,3,80,512]{3,2,1,0:T(8,128)}) %reduce-scatter.5.cloned.1.call-update) | async-done | bytes 491536 | tf_op jit(solution)/shard_map/reduce_scatter | solution.py:25
  392.5 1.1 fusion.1
  393.6 2.7 fusion.3
  396.3 0.5 copy.19
  396.9 43.8 %all_to_all.15 = f32[16,3,512,32]{2,3,1,0:T(8,128)S(1)} all-to-all(f32[16,3,512,32]{2,3,1,0:T(8,128)S(1)} %bitcast.46), channel_id=1, replica_groups=mesh['prow'=16,'pcol_0'=4,'pcol_1'=2,'pcol_2'=2] {'pcol_0','pcol_1','pco..., dimensions={0} | all-to-all | bytes 6291456 | tf_op jit(solution)/shard_map/all_to_all | solution.py:30
  440.7 0.3 reduce_sum.18
  441.2 0.4 copy.15
  441.6 0.3 reshape.143
  441.9 19.1 %all_to_all.16 = f32[16,1,3072]{2,1,0:T(1,128)S(1)} all-to-all(f32[16,1,3072]{2,1,0:T(1,128)S(1)} %reshape.143), channel_id=1, replica_groups=mesh['prow'=16,'pcol_0'=4,'pcol_1'=2,'pcol_2'=2] {'prow'}, dimensions={0} | all-to-all | bytes 393216 | tf_op jit(solution)/shard_map/all_to_all | solution.py:30
  461.0 0.5 broadcast.82
  461.5 1.1 reduce.9
  462.6 0.2 reshape.144
  463.0 0.6 sub.3
  (11 shorter events, 0.5 us)
Async XLA Ops:
  13.3 188.1 %all-to-all-start = ((f32[16,3,80,512]{3,2,1,0:T(8,128)}), f32[16,3,80,512]{3,2,1,0:T(8,128)}, u32[]{:S(2)}, u32[]{:S(2)}) async-start(f32[16,3,80,512]{3,2,1,0:T(8,128)} %stack.2), calls=%async_computation | async-start | bytes 15728640 | tf_op jit(solution)/shard_map/all_to_all | solution.py:52
  24.5 276.1 %reduce-scatter.3.cloned.1.call-start = ((), (), s32[]{:S(2)}) async-start(), calls=%async_computation.5 | async-start | bytes 11796480 | tf_op jit(solution)/shard_map/reduce_scatter | solution.py:24
  273.4 119.1 %reduce-scatter.5.cloned.1.call-start = ((), (), s32[]{:S(2)}) async-start(), calls=%async_computation.6 | async-start | bytes 4423680 | tf_op jit(solution)/shard_map/reduce_scatter | solution.py:25
  393.6 2.7 copy-start
  441.2 21.7 %copy-start.1 = (f32[3,32,32]{2,1,0:T(8,128)S(1)}, f32[3,32,32]{2,1,0:T(8,128)}, u32[]{:S(2)}) copy-start(f32[3,32,32]{2,1,0:T(8,128)} %param.19) | copy-start | bytes 36868
Sparse Core Ops, SparseCore 0:
  273.5 27.1 reduce-scatter.2
  303.2 89.1 reduce-scatter.4
